TPU v7x, 128 devices: a whole 4x4x4 slice. The times are simulated.
128 devices in a mesh: row: 8 (over x, core), col: 16 (over y, z).
Axes of the slice: x: 4, y: 4, z: 4, core: 2. Of those that a mesh axis runs over, the one named last changes fastest.
Arguments:
- left_factor: bfloat16 [4, 2048, 24, 4096], P(None, 'row', None, 'col'), may hold values from -0.01953125 to 0.01953125
- prev_solution: bfloat16 [24, 4096, 512], P('row', 'col'), may hold values from -6 to 6
- cross: bfloat16 [4, 2048, 512], P(None, 'row'), may hold values from -6 to 6
- inverses: bfloat16 [2, 2, 2048, 1, 4096], P(None, None, 'row', None, 'col'), as said below
- coupling: bfloat16 [2, 2048, 1, 4096], P(None, 'row', None, 'col'), may hold values from -0.09375 to 0.09375
- prior_cov: float32 [512, 512], P('col'), may hold values from -6 to 6
Outputs:
- solved: bfloat16 [4, 2048, 512], P(None, 'row')
- pred_cov: float32 [512, 512], P('col')
Inputs may be any that keep to these rules, and one draw needn't show every extreme that they name: Each block of inverses is lower triangular in natural order, with diagonal entries from 0.5 to 1.5.
All inputs are finite; a program needn't handle non-finite values.
Results may differ from a plain program's by a relative error of at most 0.0056.
Values may be sent and summed in bfloat16 or wider, within the bound.
No kernel may reach another device: no remote copies, remote signals or barrier semaphores. Data moves between devices by JAX's collectives and lax.ppermute only.
A program may use at most 64 MiB of HBM per device.

v0:
```python
import jax
import jax.numpy as jnp
from jax import lax
from jax.sharding import PartitionSpec as P

S = 8192


def from_root(shard, axis, root):
    return lax.dynamic_index_in_dim(lax.all_gather(shard, axis), root, 0, keepdims=False)


def filled_up(lines, peers):
    spare = -len(lines) % peers
    return jnp.pad(lines, [(0, spare)] + [(0, 0)] * (lines.ndim - 1))


def in_order(blocks, dim):
    shape = list(blocks.shape[1:])
    shape[dim] *= blocks.shape[0]
    return jnp.moveaxis(blocks, 0, dim).reshape(shape)


def from_everyone(shard, axis):
    peers = lax.axis_size(axis)
    return lax.all_to_all(
        jnp.broadcast_to(shard[None], (peers, *shard.shape)), axis, 0, 0, tiled=True
    )


def gather_directly(shard, axis, dim):
    return in_order(from_everyone(shard, axis), dim)


def cut_along(shard, dim, peers):
    shape = shard.shape
    blocks = shard.reshape(*shape[:dim], peers, shape[dim] // peers, *shape[dim + 1 :])
    return jnp.moveaxis(blocks, dim, 0)


def sent_and_summed(shard, axis, dim):
    blocks = cut_along(shard, dim, lax.axis_size(axis))
    arrived = lax.all_to_all(blocks, axis, split_axis=0, concat_axis=0, tiled=True)
    return arrived.sum(axis=0)


def sum_by_parts(shard, axes):
    lines = shard.reshape(-1, shard.shape[-1])
    padded = filled_up(lines, lax.axis_size(axes))
    whole = gather_directly(sent_and_summed(padded, axes, 0), axes, 0)
    return lax.slice_in_dim(whole, 0, len(lines)).reshape(shard.shape)


def over_copies(shard, axis):
    return from_everyone(shard, axis).astype(jnp.float32).sum(axis=0)


def apply_block(matrix, values):
    return jnp.einsum("atbu,bum->atm", matrix, values, preferred_element_type=jnp.float32)


def spread_rows(values):
    n_row = lax.axis_size("row")
    n_col = lax.axis_size("col")
    col_id = lax.axis_index("col")
    rounds, tile, sites = values.shape
    group = n_col // n_row
    grouped = values.reshape(rounds // group, group, tile, sites)
    picked = lax.dynamic_index_in_dim(grouped, col_id // n_row, 1, keepdims=False)
    return from_root(picked, "row", col_id % n_row)


def column_sum(values):
    return sum_by_parts(values, "col")


def solve_rounded(values):
    return sum_by_parts(values, "col").astype(jnp.bfloat16)


def outer_rows(solution):
    share = solution.shape[2] // lax.axis_size("col")
    own = lax.dynamic_slice_in_dim(solution, lax.axis_index("col") * share, share, 2)
    return jnp.einsum("atm,atn->mn", own, solution, preferred_element_type=jnp.float32)


def body(left_factor, prev_solution, cross, inverses, coupling, prior_cov):
    half = coupling.shape[0]
    pre = jnp.einsum(
        "atbu,bum->atm",
        left_factor,
        lax.all_gather(prev_solution, "row", axis=0, tiled=True),
        preferred_element_type=jnp.float32,
    )
    cross_first = cross[:half].astype(jnp.float32)
    cross_second = cross[half:].astype(jnp.float32)
    pre_first = sum_by_parts(pre[:half], "col")
    first_rhs = (cross_first - pre_first).astype(jnp.bfloat16)
    solved_first = solve_rounded(apply_block(inverses[0], spread_rows(first_rhs)))
    linked = column_sum(pre[half:] + apply_block(coupling, spread_rows(solved_first)))
    second_rhs = (cross_second - linked).astype(jnp.bfloat16)
    solved_second = solve_rounded(apply_block(inverses[1], spread_rows(second_rhs)))
    solved_all = jnp.concatenate([solved_first, solved_second], axis=0)
    outer_total = over_copies(outer_rows(solved_all).astype(jnp.bfloat16), "row").astype(
        jnp.float32
    )
    pred_cov = prior_cov - outer_total / S
    return (solved_all, pred_cov)


def solution(mesh):
    placed = (
        P(None, "row", None, "col"),
        P("row", "col", None),
        P(None, "row", None),
        P(None, None, "row", None, "col"),
        P(None, "row", None, "col"),
        P("col", None),
    )
    return jax.shard_map(
        body,
        mesh=mesh,
        in_specs=placed,
        out_specs=(P(None, "row", None), P("col", None)),
        check_vma=False,
    )
```

profile of v0, /device:TPU:1, one launch (start us, length us, event | category | flops | bytes accessed | tf_op | source)
XLA Modules:
  0.0 326.6 jit_solution(15073894378876235162)
XLA Ops:
  7.2 0.0 copy-start
  7.2 0.0 all-gather.8.cloned.1.call-start
  7.2 0.7 all-gather.8.cloned.1.call-update
  7.9 46.3 %all-gather.8.cloned.1.call-done = bf16[24,256,512]{2,1,0:T(8,128)(2,1)} async-done(((bf16[3,256,512]{2,1,0:T(8,128)(2,1)}), bf16[24,256,512]{2,1,0:T(8,128)(2,1)}) %all-gather.8.cloned.1.call-update) | async-done | bytes 6291472 | tf_op jit(solution)/shard_map/all_gather | solution.py:92
  54.2 14.2 %fusion.3 = f32[4,256,512]{2,1,0:T(8,128)S(1)} fusion(bf16[24,256,512]{2,1,0:T(8,128)(2,1)} %all-gather.8.cloned.1.call-done, bf16[4,256,24,256]{3,2,1,0:T(8,128)(2,1)} %param.6), kind=kOutput, calls=%fused_computation.3 | convolution fusion | flops 6442450944 | bytes 20971520 | tf_op jit(solution)/shard_map/atbu,bum->atm/dot_general | solution.py:89
  68.4 0.1 slice.24
  68.5 22.4 %all_to_all.45 = f32[16,32,512]{2,1,0:T(8,128)S(1)} all-to-all(f32[16,32,512]{2,1,0:T(8,128)S(1)} %bitcast.52), channel_id=1, replica_groups=mesh['row'=8,'col'=16] {'col'}, dimensions={0} | all-to-all | bytes 2097152 | tf_op jit(solution)/shard_map/all_to_all | solution.py:43
  90.9 0.1 reduce_sum.45
  91.0 1.1 broadcast_in_dim.10
  92.1 3.9 %all-to-all-start.1 = ((f32[16,32,512]{2,1,0:T(8,128)}), f32[16,32,512]{2,1,0:T(8,128)S(1)}, u32[]{:S(2)}, u32[]{:S(2)}) async-start(f32[16,32,512]{2,1,0:T(8,128)} %broadcast_in_dim.10), calls=%async_computation.1 | async-start | bytes 2097152 | tf_op jit(solution)/shard_map/all_to_all | solution.py:26
  96.0 0.0 all-gather.10.cloned.1.call-start
  96.1 2.3 fusion.26
  98.4 12.7 %all-to-all-done.1 = f32[16,32,512]{2,1,0:T(8,128)S(1)} async-done(((f32[16,32,512]{2,1,0:T(8,128)}), f32[16,32,512]{2,1,0:T(8,128)S(1)}, u32[]{:S(2)}, u32[]{:S(2)}) %all-to-all-start.1) | async-done | bytes 1048608 | tf_op jit(solution)/shard_map/all_to_all | solution.py:26
  111.0 1.7 fusion.11
  112.8 0.0 all-gather.10.cloned.1.call-update
  112.8 0.0 all-gather.12.cloned.1.call-start
  112.9 1.8 fusion.27
  114.6 22.8 %all-gather.10.cloned.1.call-done = bf16[8,256,512]{2,1,0:T(8,128)(2,1)} async-done(((bf16[1,256,512]{2,1,0:T(8,128)(2,1)}), bf16[8,256,512]{2,1,0:T(8,128)(2,1)}) %all-gather.10.cloned.1.call-update) | async-done | bytes 2097168 | tf_op jit(solution)/shard_map/all_gather | solution.py:10
  137.5 1.2 convolution_bitcast_fusion.2
  138.7 22.4 %all_to_all.46 = f32[16,32,512]{2,1,0:T(8,128)S(1)} all-to-all(f32[16,32,512]{2,1,0:T(8,128)S(1)} %convolution_bitcast_fusion.2), channel_id=1, replica_groups=mesh['row'=8,'col'=16] {'col'}, dimensions={0} | all-to-all | bytes 2097152 | tf_op jit(solution)/shard_map/all_to_all | solution.py:43
  161.1 0.1 reduce_sum.46
  161.3 12.8 %all_to_all.47 = bf16[16,32,512]{2,1,0:T(8,128)(2,1)S(1)} all-to-all(bf16[16,32,512]{2,1,0:T(8,128)(2,1)S(1)} %broadcast_in_dim.11), channel_id=1, replica_groups=mesh['row'=8,'col'=16] {'col'}, dimensions={0} | all-to-all | bytes 1048576 | tf_op jit(solution)/shard_map/all_to_all | solution.py:26
  174.0 0.7 constant_dynamic-slice_fusion
  174.7 0.0 all-gather.12.cloned.1.call-update
  174.8 0.0 all-gather.14.cloned.1.call-start
  174.8 25.1 %all-gather.12.cloned.1.call-done = bf16[8,256,512]{2,1,0:T(8,128)(2,1)} async-done(((bf16[1,256,512]{2,1,0:T(8,128)(2,1)}), bf16[8,256,512]{2,1,0:T(8,128)(2,1)}) %all-gather.12.cloned.1.call-update) | async-done | bytes 2097168 | tf_op jit(solution)/shard_map/all_gather | solution.py:10
  199.9 0.0 copy-done
  199.9 1.2 fusion.8
  201.2 22.4 %all_to_all.48 = f32[16,32,512]{2,1,0:T(8,128)S(1)} all-to-all(f32[16,32,512]{2,1,0:T(8,128)S(1)} %bitcast.51), channel_id=1, replica_groups=mesh['row'=8,'col'=16] {'col'}, dimensions={0} | all-to-all | bytes 2097152 | tf_op jit(solution)/shard_map/all_to_all | solution.py:43
  223.6 0.0 copy-start.2
  223.6 0.1 reduce_sum.47
  223.7 0.0 copy-start.3
  223.7 0.1 broadcast_in_dim.12
  223.8 18.5 %all_to_all.49 = f32[16,32,512]{2,1,0:T(8,128)S(1)} all-to-all(f32[16,32,512]{2,1,0:T(8,128)S(1)} %broadcast_in_dim.12), channel_id=1, replica_groups=mesh['row'=8,'col'=16] {'col'}, dimensions={0} | all-to-all | bytes 2097152 | tf_op jit(solution)/shard_map/all_to_all | solution.py:26
  242.3 0.0 copy-done.2
  242.3 0.8 fusion.10
  243.1 0.0 all-gather.14.cloned.1.call-update
  243.1 25.2 %all-gather.14.cloned.1.call-done = bf16[8,256,512]{2,1,0:T(8,128)(2,1)} async-done(((bf16[1,256,512]{2,1,0:T(8,128)(2,1)}), bf16[8,256,512]{2,1,0:T(8,128)(2,1)}) %all-gather.14.cloned.1.call-update) | async-done | bytes 2097168 | tf_op jit(solution)/shard_map/all_gather | solution.py:10
  268.3 0.0 copy-done.3
  268.3 1.2 convolution_bitcast_fusion
  269.6 22.4 %all_to_all.50 = f32[16,32,512]{2,1,0:T(8,128)S(1)} all-to-all(f32[16,32,512]{2,1,0:T(8,128)S(1)} %convolution_bitcast_fusion), channel_id=1, replica_groups=mesh['row'=8,'col'=16] {'col'}, dimensions={0} | all-to-all | bytes 2097152 | tf_op jit(solution)/shard_map/all_to_all | solution.py:43
  292.0 0.1 reduce_sum.48
  292.1 0.8 broadcast_in_dim.13
  292.9 3.9 %all-to-all-start.7 = ((bf16[16,32,512]{2,1,0:T(8,128)(2,1)}), bf16[16,32,512]{2,1,0:T(8,128)(2,1)S(1)}, u32[]{:S(2)}, u32[]{:S(2)}) async-start(bf16[16,32,512]{2,1,0:T(8,128)(2,1)} %broadcast_in_dim.13), calls=%async_computation.7 | async-start | bytes 1048576 | tf_op jit(solution)/shard_map/all_to_all | solution.py:26
  296.8 9.1 %all-to-all-done.7 = bf16[16,32,512]{2,1,0:T(8,128)(2,1)S(1)} async-done(((bf16[16,32,512]{2,1,0:T(8,128)(2,1)}), bf16[16,32,512]{2,1,0:T(8,128)(2,1)S(1)}, u32[]{:S(2)}, u32[]{:S(2)}) %all-to-all-start.7) | async-done | bytes 524320 | tf_op jit(solution)/shard_map/all_to_all | solution.py:26
  306.0 0.1 pad_maximum_fusion
  306.1 0.0 copy-start.1
  306.1 0.0 copy-start.4
  306.1 0.4 fusion.9
  306.6 12.9 %all_to_all.51 = bf16[8,32,512]{2,1,0:T(8,128)(2,1)S(1)} all-to-all(bf16[8,32,512]{2,1,0:T(8,128)(2,1)S(1)} %broadcast_in_dim.14), channel_id=1, replica_groups=mesh['row'=8,'col'=16] {'row'}, dimensions={0} | all-to-all | bytes 524288 | tf_op jit(solution)/shard_map/all_to_all | solution.py:26
  319.5 0.0 copy-done.4
  319.5 0.6 multiply_subtract_fusion
  320.1 0.0 copy-done.1
  (3 shorter events, 0.1 us)
Async XLA Ops:
  7.2 192.8 %copy-start = (bf16[2,256,1,256]{3,1,2,0:T(8,128)(2,1)S(1)}, bf16[2,256,1,256]{3,1,2,0:T(8,128)(2,1)}, u32[]{:S(2)}) copy-start(bf16[2,256,1,256]{3,1,2,0:T(8,128)(2,1)} %param.10) | copy-start | bytes 786436
  7.2 47.1 %all-gather.8.cloned.1.call-start = ((), (), s32[]{:S(2)}) async-start(), calls=%async_computation.9 | async-start | bytes 7077888 | tf_op jit(solution)/shard_map/all_gather | solution.py:92
  92.1 19.0 %all-to-all-start.1 = ((f32[16,32,512]{2,1,0:T(8,128)}), f32[16,32,512]{2,1,0:T(8,128)S(1)}, u32[]{:S(2)}, u32[]{:S(2)}) async-start(f32[16,32,512]{2,1,0:T(8,128)} %broadcast_in_dim.10), calls=%async_computation.1 | async-start | bytes 2097152 | tf_op jit(solution)/shard_map/all_to_all | solution.py:26
  96.0 41.4 %all-gather.10.cloned.1.call-start = ((), (), s32[]{:S(2)}) async-start(), calls=%async_computation.10 | async-start | bytes 2359296 | tf_op jit(solution)/shard_map/all_gather | solution.py:10
  112.8 87.1 %all-gather.12.cloned.1.call-start = ((), (), s32[]{:S(2)}) async-start(), calls=%async_computation.11 | async-start | bytes 2359296 | tf_op jit(solution)/shard_map/all_gather | solution.py:10
  174.8 93.5 %all-gather.14.cloned.1.call-start = ((), (), s32[]{:S(2)}) async-start(), calls=%async_computation.12 | async-start | bytes 2359296 | tf_op jit(solution)/shard_map/all_gather | solution.py:10
  223.6 18.7 %copy-start.2 = (bf16[2,256,512]{2,1,0:T(8,128)(2,1)S(1)}, bf16[2,256,512]{2,1,0:T(8,128)(2,1)}, u32[]{:S(2)}) copy-start(bf16[2,256,512]{2,1,0:T(8,128)(2,1)} %get-tuple-element.2) | copy-start | bytes 1572868
  223.7 44.6 %copy-start.3 = (bf16[1,2,256,1,256]{4,2,3,1,0:T(8,128)(2,1)S(1)}, bf16[1,2,256,1,256]{4,2,3,1,0:T(8,128)(2,1)}, u32[]{:S(2)}) copy-start(bf16[1,2,256,1,256]{4,2,3,1,0:T(8,128)(2,1)} %get-tuple-element.5) | copy-start | bytes 786436
  292.9 13.1 %all-to-all-start.7 = ((bf16[16,32,512]{2,1,0:T(8,128)(2,1)}), bf16[16,32,512]{2,1,0:T(8,128)(2,1)S(1)}, u32[]{:S(2)}, u32[]{:S(2)}) async-start(bf16[16,32,512]{2,1,0:T(8,128)(2,1)} %broadcast_in_dim.13), calls=%async_computation.7 | async-start | bytes 1048576 | tf_op jit(solution)/shard_map/all_to_all | solution.py:26
  306.1 14.0 %copy-start.1 = (bf16[4,256,512]{2,1,0:T(8,128)(2,1)}, bf16[4,256,512]{2,1,0:T(8,128)(2,1)S(1)}, u32[]{:S(2)}) copy-start(bf16[4,256,512]{2,1,0:T(8,128)(2,1)S(1)} %pad_maximum_fusion) | copy-start | bytes 3145732
  306.1 13.4 %copy-start.4 = (f32[32,512]{1,0:T(8,128)S(1)}, f32[32,512]{1,0:T(8,128)}, u32[]{:S(2)}) copy-start(f32[32,512]{1,0:T(8,128)} %param.11) | copy-start | bytes 196612
Sparse Core Ops, SparseCore 0:
  9.7 44.4 all-gather.7
  112.9 24.4 all-gather.9
  174.9 25.0 all-gather.11
  243.2 25.0 all-gather.13
where the time goes:
time: 327 us
  waiting for transfers between devices  142 us (43%)
  blocking collectives  134 us (41%)
  matrix products  18.3 us (6%)
  between operations  13.9 us (4%)
  starting transfers between devices  8 us (2%)
  local copies, waits for them, and re-layouts  7.02 us (2%)
  other arithmetic  3.55 us (1%)
    all_to_all x4, blocking collectives, sent_and_summed(): lax.all_to_all(blocks, axis, split_axis=0, concat_axis=0, tiled=True)  89.7 us
    all_gather x3, waiting for transfers between devices, from_root(): lax.all_gather(shard, axis)  73.1 us
    all_gather x1, waiting for transfers between devices, body(): lax.all_gather(prev_solution, 'row', axis=0, tiled=True)  46.3 us
    all_to_all x3, blocking collectives, from_everyone(): lax.all_to_all(jnp.broadcast_to(shard[None], (peers, *shard.shape)), axis...  44.1 us
    all_to_all x2, waiting for transfers between devices, from_everyone(): lax.all_to_all(jnp.broadcast_to(shard[None], (peers, *shard.shape)), axis...  21.8 us
    dot_general x1, matrix products, body(): jnp.einsum('atbu,bum->atm', left_factor, lax.all_gather(prev_solution, 'r...  14.2 us
    all_to_all x2, starting transfers between devices, from_everyone(): lax.all_to_all(jnp.broadcast_to(shard[None], (peers, *shard.shape)), axis...  7.83 us
  transfers between devices with their start and end apart: 6, of which 6 were waited for; matrix products, arithmetic and copies ran while one was open for 1% of the time, Pallas kernels for 0%

commit v1 on v0

--- a/solution.py
+++ b/solution.py
@@ -89,7 +89,9 @@
     pre = jnp.einsum(
         "atbu,bum->atm",
         left_factor,
-        lax.all_gather(prev_solution, "row", axis=0, tiled=True),
+        jnp.concatenate(
+            lax.all_to_all(jnp.stack([prev_solution] * lax.axis_size("row")), "row", 0, 0), axis=0
+        ),
         preferred_element_type=jnp.float32,
     )
     cross_first = cross[:half].astype(jnp.float32)

time: 327 us -> 358 us (1.095)
  blocking collectives: 134 us -> 211 us
  waiting for transfers between devices: 142 us -> 94.7 us
    all_to_all x0 -> x1, blocking collectives: none -> 77.7 us  [body(): lax.all_to_all(jnp.stack([prev_solution] * lax.axis_size('row')), 'row',...]
    all_gather x1 -> x0, waiting for transfers between devices: 46.3 us -> none  [body(): lax.all_gather(prev_solution, 'row', axis=0, tiled=True)]
  transfers between devices with their start and end apart: 6 -> 5, of which waited for: 6 -> 5; matrix products, arithmetic and copies ran while one was open for 1% -> 1% of each run, Pallas kernels for 0% -> 0%
where the time goes in v1:
time: 358 us; the launch traced here: 357 us
  blocking collectives  211 us (59%)
  waiting for transfers between devices  94.7 us (26%)
  matrix products  16.3 us (5%)
  between operations  13.9 us (4%)
  local copies, waits for them, and re-layouts  8.83 us (2%)
  starting transfers between devices  8.43 us (2%)
    all_to_all x4, blocking collectives, sent_and_summed(): lax.all_to_all(blocks, axis, split_axis=0, concat_axis=0, tiled=True)  89.5 us
    all_to_all x1, blocking collectives, body(): lax.all_to_all(jnp.stack([prev_solution] * lax.axis_size('row')), 'row',...  77.7 us
    all_gather x3, waiting for transfers between devices, from_root(): lax.all_gather(shard, axis)  73.3 us
    all_to_all x3, blocking collectives, from_everyone(): lax.all_to_all(jnp.broadcast_to(shard[None], (peers, *shard.shape)), axis...  44 us
    all_to_all x2, waiting for transfers between devices, from_everyone(): lax.all_to_all(jnp.broadcast_to(shard[None], (peers, *shard.shape)), axis...  21.4 us
    dot_general x1, matrix products, body(): jnp.einsum('atbu,bum->atm', left_factor, jnp.concatenate(lax.all_to_all(j...  12.2 us
    all_to_all x2, starting transfers between devices, from_everyone(): lax.all_to_all(jnp.broadcast_to(shard[None], (peers, *shard.shape)), axis...  8.31 us
  transfers between devices with their start and end apart: 5, of which 5 were waited for; matrix products, arithmetic and copies ran while one was open for 1% of the time, Pallas kernels for 0%

profile of v1, /device:TPU:1, one launch (start us, length us, event | category | flops | bytes accessed | tf_op | source)
XLA Modules:
  0.0 357.1 jit_solution(7146535219173262916)
XLA Ops:
  7.2 0.0 copy-start
  7.2 1.8 stack.2
  9.0 77.7 %all_to_all.50 = bf16[8,3,256,512]{3,2,1,0:T(8,128)(2,1)S(1)} all-to-all(bf16[8,3,256,512]{3,2,1,0:T(8,128)(2,1)S(1)} %stack.2), channel_id=1, replica_groups=mesh['row'=8,'col'=16] {'row'}, dimensions={0} | all-to-all | bytes 12582912 | tf_op jit(solution)/shard_map/all_to_all | solution.py:93
  86.8 12.2 %fusion.2 = f32[4,256,512]{2,1,0:T(8,128)S(1)} fusion(bf16[24,256,512,1]{2,1,0,3:T(8,128)(2,1)S(1)} %bitcast.48, bf16[4,256,24,256]{3,2,1,0:T(8,128)(2,1)} %param.6), kind=kOutput, calls=%fused_computation.2 | convolution fusion | flops 6442450944 | bytes 20971520 | tf_op jit(solution)/shard_map/atbu,bum->atm/dot_general | solution.py:89
  98.9 0.1 slice.24
  99.0 22.2 %all_to_all.51 = f32[16,32,512]{2,1,0:T(8,128)S(1)} all-to-all(f32[16,32,512]{2,1,0:T(8,128)S(1)} %bitcast.52), channel_id=1, replica_groups=mesh['row'=8,'col'=16] {'col'}, dimensions={0} | all-to-all | bytes 2097152 | tf_op jit(solution)/shard_map/all_to_all | solution.py:43
  121.2 0.1 reduce_sum.45
  121.3 1.1 broadcast_in_dim.10
  122.4 4.4 %all-to-all-start.2 = ((f32[16,32,512]{2,1,0:T(8,128)}), f32[16,32,512]{2,1,0:T(8,128)S(1)}, u32[]{:S(2)}, u32[]{:S(2)}) async-start(f32[16,32,512]{2,1,0:T(8,128)} %broadcast_in_dim.10), calls=%async_computation.2 | async-start | bytes 2097152 | tf_op jit(solution)/shard_map/all_to_all | solution.py:26
  126.8 0.0 all-gather.7.cloned.1.call-start
  126.8 2.3 fusion.23
  129.1 12.2 %all-to-all-done.2 = f32[16,32,512]{2,1,0:T(8,128)S(1)} async-done(((f32[16,32,512]{2,1,0:T(8,128)}), f32[16,32,512]{2,1,0:T(8,128)S(1)}, u32[]{:S(2)}, u32[]{:S(2)}) %all-to-all-start.2) | async-done | bytes 1048608 | tf_op jit(solution)/shard_map/all_to_all | solution.py:26
  141.3 1.7 fusion.8
  143.1 0.0 all-gather.7.cloned.1.call-update
  143.1 0.0 all-gather.9.cloned.1.call-start
  143.1 1.8 fusion.24
  144.9 23.0 %all-gather.7.cloned.1.call-done = bf16[8,256,512]{2,1,0:T(8,128)(2,1)} async-done(((bf16[1,256,512]{2,1,0:T(8,128)(2,1)}), bf16[8,256,512]{2,1,0:T(8,128)(2,1)}) %all-gather.7.cloned.1.call-update) | async-done | bytes 2097168 | tf_op jit(solution)/shard_map/all_gather | solution.py:10
  167.9 1.2 convolution_bitcast_fusion.2
  169.1 22.4 %all_to_all.52 = f32[16,32,512]{2,1,0:T(8,128)S(1)} all-to-all(f32[16,32,512]{2,1,0:T(8,128)S(1)} %convolution_bitcast_fusion.2), channel_id=1, replica_groups=mesh['row'=8,'col'=16] {'col'}, dimensions={0} | all-to-all | bytes 2097152 | tf_op jit(solution)/shard_map/all_to_all | solution.py:43
  191.6 0.1 reduce_sum.46
  191.7 12.7 %all_to_all.53 = bf16[16,32,512]{2,1,0:T(8,128)(2,1)S(1)} all-to-all(bf16[16,32,512]{2,1,0:T(8,128)(2,1)S(1)} %broadcast_in_dim.11), channel_id=1, replica_groups=mesh['row'=8,'col'=16] {'col'}, dimensions={0} | all-to-all | bytes 1048576 | tf_op jit(solution)/shard_map/all_to_all | solution.py:26
  204.4 0.7 constant_dynamic-slice_fusion
  205.2 0.0 all-gather.9.cloned.1.call-update
  205.2 0.0 all-gather.11.cloned.1.call-start
  205.2 25.1 %all-gather.9.cloned.1.call-done = bf16[8,256,512]{2,1,0:T(8,128)(2,1)} async-done(((bf16[1,256,512]{2,1,0:T(8,128)(2,1)}), bf16[8,256,512]{2,1,0:T(8,128)(2,1)}) %all-gather.9.cloned.1.call-update) | async-done | bytes 2097168 | tf_op jit(solution)/shard_map/all_gather | solution.py:10
  230.4 0.0 copy-done
  230.4 1.2 fusion.5
  231.6 22.4 %all_to_all.54 = f32[16,32,512]{2,1,0:T(8,128)S(1)} all-to-all(f32[16,32,512]{2,1,0:T(8,128)S(1)} %bitcast.51), channel_id=1, replica_groups=mesh['row'=8,'col'=16] {'col'}, dimensions={0} | all-to-all | bytes 2097152 | tf_op jit(solution)/shard_map/all_to_all | solution.py:43
  254.0 0.0 copy-start.2
  254.0 0.1 reduce_sum.47
  254.1 0.0 copy-start.3
  254.1 0.1 broadcast_in_dim.12
  254.3 18.5 %all_to_all.55 = f32[16,32,512]{2,1,0:T(8,128)S(1)} all-to-all(f32[16,32,512]{2,1,0:T(8,128)S(1)} %broadcast_in_dim.12), channel_id=1, replica_groups=mesh['row'=8,'col'=16] {'col'}, dimensions={0} | all-to-all | bytes 2097152 | tf_op jit(solution)/shard_map/all_to_all | solution.py:26
  272.7 0.0 copy-done.2
  272.7 0.8 fusion.7
  273.5 0.0 all-gather.11.cloned.1.call-update
  273.5 25.2 %all-gather.11.cloned.1.call-done = bf16[8,256,512]{2,1,0:T(8,128)(2,1)} async-done(((bf16[1,256,512]{2,1,0:T(8,128)(2,1)}), bf16[8,256,512]{2,1,0:T(8,128)(2,1)}) %all-gather.11.cloned.1.call-update) | async-done | bytes 2097168 | tf_op jit(solution)/shard_map/all_gather | solution.py:10
  298.7 0.0 copy-done.3
  298.7 1.2 convolution_bitcast_fusion
  300.0 22.4 %all_to_all.56 = f32[16,32,512]{2,1,0:T(8,128)S(1)} all-to-all(f32[16,32,512]{2,1,0:T(8,128)S(1)} %convolution_bitcast_fusion), channel_id=1, replica_groups=mesh['row'=8,'col'=16] {'col'}, dimensions={0} | all-to-all | bytes 2097152 | tf_op jit(solution)/shard_map/all_to_all | solution.py:43
  322.4 0.1 reduce_sum.48
  322.5 0.8 broadcast_in_dim.13
  323.3 3.9 %all-to-all-start.8 = ((bf16[16,32,512]{2,1,0:T(8,128)(2,1)}), bf16[16,32,512]{2,1,0:T(8,128)(2,1)S(1)}, u32[]{:S(2)}, u32[]{:S(2)}) async-start(bf16[16,32,512]{2,1,0:T(8,128)(2,1)} %broadcast_in_dim.13), calls=%async_computation.8 | async-start | bytes 1048576 | tf_op jit(solution)/shard_map/all_to_all | solution.py:26
  327.3 9.1 %all-to-all-done.8 = bf16[16,32,512]{2,1,0:T(8,128)(2,1)S(1)} async-done(((bf16[16,32,512]{2,1,0:T(8,128)(2,1)}), bf16[16,32,512]{2,1,0:T(8,128)(2,1)S(1)}, u32[]{:S(2)}, u32[]{:S(2)}) %all-to-all-start.8) | async-done | bytes 524320 | tf_op jit(solution)/shard_map/all_to_all | solution.py:26
  336.4 0.1 pad_maximum_fusion
  336.5 0.0 copy-start.1
  336.5 0.0 copy-start.4
  336.5 0.4 fusion.6
  337.0 12.8 %all_to_all.57 = bf16[8,32,512]{2,1,0:T(8,128)(2,1)S(1)} all-to-all(bf16[8,32,512]{2,1,0:T(8,128)(2,1)S(1)} %broadcast_in_dim.14), channel_id=1, replica_groups=mesh['row'=8,'col'=16] {'row'}, dimensions={0} | all-to-all | bytes 524288 | tf_op jit(solution)/shard_map/all_to_all | solution.py:26
  349.9 0.0 copy-done.4
  349.9 0.6 multiply_subtract_fusion
  350.5 0.0 copy-done.1
  (3 shorter events, 0.1 us)
Async XLA Ops:
  7.2 223.2 %copy-start = (bf16[2,256,1,256]{3,1,2,0:T(8,128)(2,1)S(1)}, bf16[2,256,1,256]{3,1,2,0:T(8,128)(2,1)}, u32[]{:S(2)}) copy-start(bf16[2,256,1,256]{3,1,2,0:T(8,128)(2,1)} %param.10) | copy-start | bytes 786436
  122.4 19.0 %all-to-all-start.2 = ((f32[16,32,512]{2,1,0:T(8,128)}), f32[16,32,512]{2,1,0:T(8,128)S(1)}, u32[]{:S(2)}, u32[]{:S(2)}) async-start(f32[16,32,512]{2,1,0:T(8,128)} %broadcast_in_dim.10), calls=%async_computation.2 | async-start | bytes 2097152 | tf_op jit(solution)/shard_map/all_to_all | solution.py:26
  126.8 41.1 %all-gather.7.cloned.1.call-start = ((), (), s32[]{:S(2)}) async-start(), calls=%async_computation.10 | async-start | bytes 2359296 | tf_op jit(solution)/shard_map/all_gather | solution.py:10
  143.1 87.3 %all-gather.9.cloned.1.call-start = ((), (), s32[]{:S(2)}) async-start(), calls=%async_computation.11 | async-start | bytes 2359296 | tf_op jit(solution)/shard_map/all_gather | solution.py:10
  205.2 93.5 %all-gather.11.cloned.1.call-start = ((), (), s32[]{:S(2)}) async-start(), calls=%async_computation.12 | async-start | bytes 2359296 | tf_op jit(solution)/shard_map/all_gather | solution.py:10
  254.0 18.7 %copy-start.2 = (bf16[2,256,512]{2,1,0:T(8,128)(2,1)S(1)}, bf16[2,256,512]{2,1,0:T(8,128)(2,1)}, u32[]{:S(2)}) copy-start(bf16[2,256,512]{2,1,0:T(8,128)(2,1)} %get-tuple-element.2) | copy-start | bytes 1572868
  254.1 44.6 %copy-start.3 = (bf16[1,2,256,1,256]{4,2,3,1,0:T(8,128)(2,1)S(1)}, bf16[1,2,256,1,256]{4,2,3,1,0:T(8,128)(2,1)}, u32[]{:S(2)}) copy-start(bf16[1,2,256,1,256]{4,2,3,1,0:T(8,128)(2,1)} %get-tuple-element.5) | copy-start | bytes 786436
  323.3 13.1 %all-to-all-start.8 = ((bf16[16,32,512]{2,1,0:T(8,128)(2,1)}), bf16[16,32,512]{2,1,0:T(8,128)(2,1)S(1)}, u32[]{:S(2)}, u32[]{:S(2)}) async-start(bf16[16,32,512]{2,1,0:T(8,128)(2,1)} %broadcast_in_dim.13), calls=%async_computation.8 | async-start | bytes 1048576 | tf_op jit(solution)/shard_map/all_to_all | solution.py:26
  336.5 14.0 %copy-start.1 = (bf16[4,256,512]{2,1,0:T(8,128)(2,1)}, bf16[4,256,512]{2,1,0:T(8,128)(2,1)S(1)}, u32[]{:S(2)}) copy-start(bf16[4,256,512]{2,1,0:T(8,128)(2,1)S(1)} %pad_maximum_fusion) | copy-start | bytes 3145732
  336.5 13.4 %copy-start.4 = (f32[32,512]{1,0:T(8,128)S(1)}, f32[32,512]{1,0:T(8,128)}, u32[]{:S(2)}) copy-start(f32[32,512]{1,0:T(8,128)} %param.11) | copy-start | bytes 196612
Sparse Core Ops, SparseCore 0:
  143.2 24.6 all-gather.6
  205.3 25.0 all-gather.8
  273.6 25.0 all-gather.10
